TPU v7x, 32 devices: a whole 2x2x4 slice. The times are simulated.
32 devices in a mesh: parts: 2 (over x), row: 8 (over z, core), col: 2 (over y).
Axes of the slice: x: 2, y: 2, z: 4, core: 2. Of those that a mesh axis runs over, the one named last changes fastest.
Arguments:
- pair_features_map: bfloat16 [64, 1024, 512], P(None, ('parts', 'row'), 'col'), parts along dimension 1, may hold values from -6 to 6
- labels: int32 [1024, 512], P(('parts', 'row', 'col')), parts along dimension 0, may hold values from 0 to 36, as said below
- lengths: int32 [2], P('parts'), parts along dimension 0, may hold values from 256 to 512
- conv_weight: bfloat16 [3, 3, 64, 64], replicated, may hold values from -0.25 to 0.25
- conv_bias: float32 [64], replicated, may hold values from -3 to 3
- head_weight: bfloat16 [37, 64], replicated, may hold values from -2.390625 to 2.390625
- head_bias: float32 [37], replicated, may hold values from -4 to 4
Outputs:
- pair_gradient: bfloat16 [64, 1024, 512], P(None, ('parts', 'row'), 'col'), parts along dimension 1
- grad_conv_weight: float32 [6, 3, 64, 64], P('parts'), parts along dimension 0
- grad_conv_bias: float32 [128], P('parts'), parts along dimension 0
- grad_head_weight: float32 [74, 64], P('parts'), parts along dimension 0
- grad_head_bias: float32 [74], P('parts'), parts along dimension 0
- loss: float32 [2], P('parts'), parts along dimension 0
There are 2 independent parts, one for each index of `parts`. A program takes and returns all parts, laid end to end along the dimension named above; an argument that names none is the same for every part. Nothing has to cross between parts.
Inputs may be any that keep to these rules, and one draw needn't show every extreme that they name: labels[i, j] equals labels[j, i] for every pair.
All inputs are finite; a program needn't handle non-finite values.
Results may differ from a plain program's by a relative error of at most 0.0067.
Values may be sent and summed in bfloat16 or wider, within the bound.
No kernel may reach another device: no remote copies, remote signals or barrier semaphores. Data moves between devices by JAX's collectives and lax.ppermute only.
A program may use at most 128 MiB of HBM per device.

v0:
```python
import jax
import jax.numpy as jnp
from jax import lax
from jax.sharding import PartitionSpec as P

DILATION_STEP = 4


def with_halo(cells, sides, width):
    for axis, dim in sides:
        count = lax.axis_size(axis)
        ends = count - 1
        head = lax.slice_in_dim(cells, 0, width, axis=dim)
        tail = lax.slice_in_dim(cells, cells.shape[dim] - width, cells.shape[dim], axis=dim)
        cells = jnp.concatenate(
            [
                lax.ppermute(tail, axis, [(i, (i + 1) % count) for i in range(ends)]),
                cells,
                lax.ppermute(head, axis, [((i + 1) % count, i) for i in range(ends)]),
            ],
            axis=dim,
        )
    return cells


def tile_to_band(field):
    channels, patch_rows, patch_columns = field.shape
    width = lax.axis_size("col")
    split = field.reshape(channels, width, patch_rows // width, patch_columns)
    moved = lax.all_to_all(split, "col", split_axis=1, concat_axis=3, tiled=True)
    return moved.reshape(channels, patch_rows // width, width * patch_columns)


def band_to_tile(field):
    channels, band_rows, length_cols = field.shape
    width = lax.axis_size("col")
    split = field.reshape(channels, band_rows, width, length_cols // width)
    moved = lax.all_to_all(split, "col", split_axis=2, concat_axis=1, tiled=True)
    return moved.reshape(channels, width * band_rows, length_cols // width)


def reorder_back(moved, channels, band_rows, length_cols):
    return jnp.transpose(moved, (0, 3, 2, 1)).reshape(channels, band_rows, length_cols)


def mirror_features(field):
    channels, band_rows, length_cols = field.shape
    bands = lax.axis_size(("row", "col"))
    blocks = field.reshape(channels, band_rows, bands, band_rows)
    moved = lax.all_to_all(blocks, ("row", "col"), split_axis=2, concat_axis=2, tiled=True)
    return reorder_back(moved, channels, band_rows, length_cols)


def per_device(pair_features_map, labels, lengths, conv_weight, conv_bias, head_weight, head_bias):
    channels, patch_rows, patch_columns = pair_features_map.shape
    nbins = head_weight.shape[0]
    bordered_input = with_halo(pair_features_map, (("row", 1), ("col", 2)), DILATION_STEP)
    before_activation = (
        jnp.zeros((channels, patch_rows, patch_columns), jnp.float32) + conv_bias[:, None, None]
    )
    for offset_row in range(3):
        for offset_column in range(3):
            sliding_patch = bordered_input[
                :,
                DILATION_STEP * offset_row : DILATION_STEP * offset_row + patch_rows,
                DILATION_STEP * offset_column : DILATION_STEP * offset_column + patch_columns,
            ]
            before_activation = before_activation + jnp.einsum(
                "oc,cij->oij",
                conv_weight[offset_row, offset_column],
                sliding_patch,
                preferred_element_type=jnp.float32,
            )
    hidden_tile = jnp.where(
        before_activation > 0, before_activation, jnp.expm1(jnp.minimum(before_activation, 0.0))
    ).astype(jnp.bfloat16)
    hidden = tile_to_band(hidden_tile)
    band_rows, length_cols = (hidden.shape[1], hidden.shape[2])
    hidden_mirror = mirror_features(hidden)
    direct = jnp.einsum("kc,cij->kij", head_weight, hidden, preferred_element_type=jnp.float32)
    opposite = jnp.einsum(
        "kc,cij->kij", head_weight, hidden_mirror, preferred_element_type=jnp.float32
    )
    logits = 0.5 * (direct + opposite) + head_bias[:, None, None]
    band = lax.axis_index(("row", "col"))
    row_ids = band * band_rows + lax.broadcasted_iota(jnp.int32, (band_rows, length_cols), 0)
    col_ids = lax.broadcasted_iota(jnp.int32, (band_rows, length_cols), 1)
    extent = lengths[0]
    valid = ((row_ids < extent) & (col_ids < extent)).astype(jnp.float32)
    count = (extent * extent).astype(jnp.float32)
    onehot = (lax.broadcasted_iota(jnp.int32, (nbins, 1, 1), 0) == labels[None]).astype(jnp.float32)
    lse = jnp.log(jnp.sum(jnp.exp(logits), axis=0))
    picked = jnp.sum(onehot * logits, axis=0)
    loss_local = jnp.sum(valid * (lse - picked))
    dlogits = (valid[None] * (jnp.exp(logits - lse[None]) - onehot) / count).astype(jnp.bfloat16)
    head_grad = jnp.einsum("kij,cij->kc", dlogits, hidden, preferred_element_type=jnp.float32)
    head_bias_grad = jnp.sum(dlogits.astype(jnp.float32), axis=(1, 2))
    tile_grad = band_to_tile(dlogits)
    back = jnp.einsum("kc,kij->cij", head_weight, tile_grad, preferred_element_type=jnp.float32)
    slope = jnp.where(before_activation > 0, 1.0, jnp.exp(jnp.minimum(before_activation, 0.0)))
    preact_gradient = (back * slope).astype(jnp.bfloat16)
    preact_gradient_bordered = with_halo(preact_gradient, (("row", 1), ("col", 2)), DILATION_STEP)
    grad_field = jnp.zeros((channels, patch_rows, patch_columns), jnp.float32)
    tap_rows = []
    for offset_row in range(3):
        tap_cols = []
        for offset_column in range(3):
            sliding_patch = bordered_input[
                :,
                DILATION_STEP * offset_row : DILATION_STEP * offset_row + patch_rows,
                DILATION_STEP * offset_column : DILATION_STEP * offset_column + patch_columns,
            ]
            tap_cols.append(
                jnp.einsum(
                    "oij,cij->oc",
                    preact_gradient,
                    sliding_patch,
                    preferred_element_type=jnp.float32,
                )
            )
            row_begin = DILATION_STEP * (2 - offset_row)
            column_begin = DILATION_STEP * (2 - offset_column)
            source = preact_gradient_bordered[
                :, row_begin : row_begin + patch_rows, column_begin : column_begin + patch_columns
            ]
            grad_field = grad_field + jnp.einsum(
                "oc,oij->cij",
                conv_weight[offset_row, offset_column],
                source,
                preferred_element_type=jnp.float32,
            )
        tap_rows.append(jnp.stack(tap_cols))
    conv_grad = jnp.stack(tap_rows)
    conv_bias_grad = jnp.sum(preact_gradient.astype(jnp.float32), axis=(1, 2))
    conv_grad, conv_bias_grad, head_grad, head_bias_grad, loss_total = lax.psum(
        (conv_grad, conv_bias_grad, head_grad, head_bias_grad, loss_local), ("row", "col")
    )
    loss = (loss_total / count).reshape(1)
    return (
        grad_field.astype(jnp.bfloat16),
        conv_grad,
        conv_bias_grad,
        head_grad,
        head_bias_grad,
        loss,
    )


def solution(mesh):
    return jax.shard_map(
        per_device,
        mesh=mesh,
        in_specs=(
            P(None, ("parts", "row"), "col"),
            P(("parts", "row", "col"), None),
            P("parts"),
            P(),
            P(),
            P(),
            P(),
        ),
        out_specs=(
            P(None, ("parts", "row"), "col"),
            P("parts", None, None, None),
            P("parts"),
            P("parts", None),
            P("parts"),
            P("parts"),
        ),
        check_vma=False,
    )
```

profile of v0, /device:TPU:0, one launch (start us, length us, event | category | flops | bytes accessed | tf_op | source)
XLA Modules:
  0.0 410.8 jit_solution(8611053157606536604)
XLA Ops:
  13.8 4.4 %fusion.60 = f32[64,64,256]{2,0,1:T(8,128)} fusion(bf16[3,3,64,64]{3,2,1,0:T(8,128)(2,1)} %param.10, bf16[64,64,256]{2,1,0:T(8,128)(2,1)S(1)} %copy-done.10), kind=kOutput, calls=%fused_computation.100 | convolution fusion | flops 134217728 | bytes 6307840 | tf_op jit(solution)/shard_map/oc,cij->oij/dot_general | solution.py:68
  25.1 4.9 %collective-permute-start.2 = (bf16[64,72,4]{1,0,2:T(8,128)(2,1)}, bf16[64,72,4]{1,0,2:T(8,128)(2,1)}, u32[]{:S(2)}, u32[]{:S(2)}) collective-permute-start(bf16[64,72,4]{1,0,2:T(8,128)(2,1)} %copy.58), channel_id=1, source_target_pairs={{0,1},{2,3},{4,5},{6,7},{8,9},{10,11},{12,13},{14,15},{16,17},{18,... | collective-permute-start | bytes 110600 | tf_op jit(solution)/shard_map/ppermute | solution.py:17
  33.7 4.3 %fusion.41 = f32[64,256,64]{1,2,0:T(8,128)} fusion(bf16[64,64,256]{2,0,1:T(8,128)(2,1)} %copy-done.7, bf16[64,4,256]{2,0,1:T(8,128)(2,1)} %copy-done.23, bf16[3,3,64,64]{3,2,1,0:T(8,128)(2,1)} %param.10), kind=kOutput, calls=%fused_computation.67 | convolution fusion | flops 138412032 | bytes 6438912 | tf_op jit(solution)/shard_map/oc,cij->oij/dot_general | solution.py:68
  58.1 3.9 fusion.56
  65.9 13.3 %fusion = (bf16[64,64,256]{2,0,1:T(8,128)(2,1)S(1)}, f32[64,64,256]{2,0,1:T(8,128)}) fusion(bf16[64,72,4]{2,0,1:T(8,128)(2,1)S(1)} %copy.62, bf16[64,72,256]{2,0,1:T(8,128)(2,1)S(1)} %constant_dynamic-update-slice_fusion, bf16[3,3,64,64]{3,2,1,0:T(8,128)(2,1)} %param.10, f32[64,256,64]{1,2,0:T(8,128)} %fusion.43, f32[64,256,64]{1,2,0:T(8,128)} %fusion.47, ...), kind=kOutput, calls=%fused_computation.6 | convolution fusion | flops 152043520 | bytes 42258688 | tf_op jit(solution)/shard_map/oc,cij->oij/dot_general | solution.py:68
  80.4 29.7 %all_to_all.35 = bf16[64,2,32,256]{3,2,0,1:T(8,128)(2,1)} all-to-all(bf16[64,2,32,256]{3,2,0,1:T(8,128)(2,1)S(1)} %copy.65), channel_id=1, replica_groups=mesh['parts'=2,'row'=8,'col'=2] {'col'}, dimensions={1} | all-to-all | bytes 4194304 | tf_op jit(solution)/shard_map/all_to_all | solution.py:30
  110.1 5.0 %copy.66 = bf16[64,2,32,256]{0,3,1,2:T(8,128)(2,1)} copy(bf16[64,2,32,256]{3,2,0,1:T(8,128)(2,1)} %all_to_all.35) | data formatting | bytes 4194304 | tf_op jit(solution)/shard_map/all_to_all | solution.py:30
  115.0 5.3 %copy.126 = bf16[64,32,16,32]{0,3,1,2:T(8,128)(2,1)} copy(bf16[64,32,16,32]{0,3,2,1:T(8,128)(2,1)} %bitcast.202) | data formatting | bytes 4194304 | tf_op jit(solution)/shard_map/reshape;reshape | solution.py:49
  120.3 7.5 %reshape.99 = bf16[16,2,32768]{2,1,0:T(2,128)(2,1)} reshape(bf16[16,32,32,64]{3,2,1,0:T(8,128)(2,1)} %bitcast.205) | data formatting | bytes 4194304
  127.9 6.9 %all-to-all-start.1 = ((bf16[16,2,32768]{2,1,0:T(2,128)(2,1)}), bf16[16,2,32768]{2,1,0:T(2,128)(2,1)}, u32[]{:S(2)}, u32[]{:S(2)}) async-start(bf16[16,2,32768]{2,1,0:T(2,128)(2,1)} %reshape.99), calls=%async_computation.1 | async-start | bytes 4194304 | tf_op jit(solution)/shard_map/all_to_all | solution.py:50
  136.7 6.1 %fusion.93 = f32[32,512,37]{1,2,0:T(8,128)} fusion(bf16[64,32,512]{0,2,1:T(8,128)(2,1)} %bitcast.203, bf16[37,64]{1,0:T(8,128)(2,1)S(1)} %copy-done), kind=kOutput, calls=%fused_computation.133 | convolution fusion | flops 77594624 | bytes 4526720 | tf_op jit(solution)/shard_map/kc,cij->kij/dot_general | solution.py:80
  142.9 34.0 %all-to-all-done.1 = bf16[16,2,32768]{2,1,0:T(2,128)(2,1)} async-done(((bf16[16,2,32768]{2,1,0:T(2,128)(2,1)}), bf16[16,2,32768]{2,1,0:T(2,128)(2,1)}, u32[]{:S(2)}, u32[]{:S(2)}) %all-to-all-start.1) | async-done | bytes 2097184 | tf_op jit(solution)/shard_map/all_to_all | solution.py:50
  176.9 7.4 %reshape.100 = bf16[16,32,32,64]{3,2,1,0:T(8,128)(2,1)} reshape(bf16[16,2,32768]{2,1,0:T(2,128)(2,1)} %all-to-all-done.1) | data formatting | bytes 4194304
  184.3 7.9 %fusion.10 = (f32[32,512]{1,0:T(8,128)S(1)}, f32[32,512]{1,0:T(8,128)S(1)}, f32[32,512,37]{1,2,0:T(8,128)S(1)}) fusion(s32[32,512]{1,0:T(8,128)} %param.8, f32[37]{0:T(128)} %param.13, f32[32,512,37]{1,2,0:T(8,128)} %fusion.93, bf16[37,64]{1,0:T(8,128)(2,1)S(1)} %copy-done, bf16[64,32,512]{0,1,2:T(8,128)(2,1)} %bitcast.207), kind=kOutput, calls=%fused_computation.32 | convolution fusion | flops 81805312 | bytes 7148308 | tf_op jit(solution)/shard_map/kc,cij->kij/dot_general | solution.py:81
  201.5 4.5 %all-to-all-start.2 = ((bf16[37,32,2,256]{3,1,0,2:T(8,128)(2,1)}), bf16[37,32,2,256]{3,1,0,2:T(8,128)(2,1)}, u32[]{:S(2)}, u32[]{:S(2)}) async-start(bf16[37,32,2,256]{3,1,0,2:T(8,128)(2,1)} %copy.72), calls=%async_computation.2 | async-start | bytes 2424832 | tf_op jit(solution)/shard_map/all_to_all | solution.py:38
  206.2 4.1 convolution_bitcast_fusion.7
  210.3 10.8 %all-to-all-done.2 = bf16[37,32,2,256]{3,1,0,2:T(8,128)(2,1)} async-done(((bf16[37,32,2,256]{3,1,0,2:T(8,128)(2,1)}), bf16[37,32,2,256]{3,1,0,2:T(8,128)(2,1)}, u32[]{:S(2)}, u32[]{:S(2)}) %all-to-all-start.2) | async-done | bytes 1212448 | tf_op jit(solution)/shard_map/all_to_all | solution.py:38
  223.1 4.2 %convert_reduce_fusion = (f32[64]{0:T(128)}, bf16[64,64,256]{2,0,1:T(8,128)(2,1)S(1)}) fusion(f32[64,64,256]{2,0,1:T(8,128)} %get-tuple-element.45, bf16[37,64,256]{2,0,1:T(8,128)(2,1)S(1)} %bitcast.208, bf16[37,64]{1,0:T(8,128)(2,1)S(1)} %copy-done), kind=kOutput, calls=%fused_computation.17 | convolution fusion | flops 84934592 | bytes 7508864 | tf_op jit(solution)/shard_map/kc,kij->cij/dot_general | solution.py:99
  243.0 4.4 %collective-permute-start.4 = (bf16[64,4,256]{2,0,1:T(8,128)(2,1)S(1)}, bf16[64,4,256]{2,0,1:T(8,128)(2,1)S(1)}, u32[]{:S(2)}, u32[]{:S(2)}) collective-permute-start(bf16[64,4,256]{2,0,1:T(8,128)(2,1)S(1)} %get-tuple-element.39), channel_id=1, source_target_pairs={{0,2},{2,4},{4,6},{6,8},{8,10},{10,12},{12,14},{1,3},{3,5},{5,7},{... | collective-permute-start | bytes 393224 | tf_op jit(solution)/shard_map/ppermute | solution.py:17
  249.0 62.7 %all-reduce = (f32[64]{0:T(128)}, f32[37,64]{1,0:T(8,128)}, f32[37]{0:T(128)}, f32[]{:T(128)}) all-reduce(f32[64]{0:T(128)S(1)} %copy-done.30, f32[37,64]{1,0:T(8,128)S(1)} %copy-done.26, f32[37]{0:T(128)S(1)} %get-tuple-element.30, f32[]{:T(128)} %get-tuple-element.42), channel_id=1, replica_groups=mesh['parts'=2,'row'=8,'col'=2] {'row','col'}, use_global_device_ids=true, to_apply=%region_3.4 | all-reduce | flops 2470 | bytes 19760 | tf_op jit(solution)/shard_map/psum | solution.py:135
  324.1 5.9 %collective-permute-start.7 = (bf16[64,72,4]{1,0,2:T(8,128)(2,1)}, bf16[64,72,4]{1,0,2:T(8,128)(2,1)}, u32[]{:S(2)}, u32[]{:S(2)}) collective-permute-start(bf16[64,72,4]{1,0,2:T(8,128)(2,1)} %copy.78), channel_id=1, source_target_pairs={{0,1},{2,3},{4,5},{6,7},{8,9},{10,11},{12,13},{14,15},{16,17},{18,... | collective-permute-start | bytes 110600 | tf_op jit(solution)/shard_map/ppermute | solution.py:17
  343.5 6.5 %maximum_maximum_fusion = (bf16[64,72,260]{2,0,1:T(8,128)(2,1)S(1)}, bf16[64,72,260]{2,0,1:T(8,128)(2,1)S(1)}) fusion(bf16[64,4,256]{2,0,1:T(8,128)(2,1)S(1)} %copy-done.16, bf16[64,64,256]{2,0,1:T(8,128)(2,1)S(1)} %copy-done.3, bf16[64,4,256]{2,0,1:T(8,128)(2,1)S(1)} %copy-done.18, bf16[64,72,4]{2,0,1:T(8,128)(2,1)} %copy.79, bf16[64,72,4]{2,0,1:T(8,128)(2,1)S(1)} %copy.75), kind=kLoop, calls=%fused_computation.23 | loop fusion | flops 19169280 | bytes 7225344 | tf_op jit(solution)/shard_map/concatenate | solution.py:15
  364.3 10.8 %fusion.24 = bf16[64,64,256]{2,0,1:T(8,128)(2,1)S(1)} fusion(f32[64,256,64]{1,2,0:T(8,128)} %fusion.16, f32[64,256,64]{1,2,0:T(8,128)} %fusion.29, f32[64,256,64]{1,2,0:T(8,128)} %fusion.31, f32[64,256,64]{1,2,0:T(8,128)S(1)} %copy-done.12, f32[64,256,64]{1,2,0:T(8,128)} %fusion.33, f32[64,256,64]{1,2,0:T(8,128)} %fusion.35, f32[64,256,64]{1,2,0:T(8,128)} %fusion.37, ...), kind=kOutput, calls=%fused_computation.50 | convolution fusion | flops 143654912 | bytes 37765120 | tf_op jit(solution)/shard_map/oc,oij->cij/dot_general | solution.py:126
  377.5 23.2 %all-reduce.3.cloned.1.call-done = f32[3,3,64,64]{3,2,1,0:T(8,128)} async-done(((f32[3,3,64,64]{3,2,1,0:T(8,128)}), f32[3,3,64,64]{3,2,1,0:T(8,128)}) %all-reduce.3.cloned.1.call-update) | async-done | bytes 147472 | tf_op jit(solution)/shard_map/psum | solution.py:135
  (132 shorter events, 115.8 us)
Async XLA Ops:
  7.2 129.6 %copy-start = (bf16[37,64]{1,0:T(8,128)(2,1)S(1)}, bf16[37,64]{1,0:T(8,128)(2,1)}, u32[]{:S(2)}) copy-start(bf16[37,64]{1,0:T(8,128)(2,1)} %param.12) | copy-start | bytes 14212
  7.2 6.6 %copy-start.10 = (bf16[64,64,256]{2,1,0:T(8,128)(2,1)S(1)}, bf16[64,64,256]{2,1,0:T(8,128)(2,1)}, u32[]{:S(2)}) copy-start(bf16[64,64,256]{2,1,0:T(8,128)(2,1)} %param.7) | copy-start | bytes 6291460
  10.1 8.1 %copy-start.7 = (bf16[64,64,256]{2,0,1:T(8,128)(2,1)}, bf16[64,64,256]{2,0,1:T(8,128)(2,1)S(1)}, u32[]{:S(2)}) copy-start(bf16[64,64,256]{2,0,1:T(8,128)(2,1)S(1)} %copy.55) | copy-start | bytes 6291460
  10.2 8.1 %collective-permute-start = (bf16[64,4,256]{2,0,1:T(8,128)(2,1)S(1)}, bf16[64,4,256]{2,0,1:T(8,128)(2,1)S(1)}, u32[]{:S(2)}, u32[]{:S(2)}) collective-permute-start(bf16[64,4,256]{2,0,1:T(8,128)(2,1)S(1)} %get-tuple-element.40), channel_id=1, source_target_pairs={{0,2},{2,4},{4,6},{6,8},{8,10},{10,12},{12,14},{1,3},{3,5},{5,7},{... | collective-permute-start | bytes 393224 | tf_op jit(solution)/shard_map/ppermute | solution.py:17
  12.5 6.9 %collective-permute-start.1 = (bf16[64,4,256]{2,0,1:T(8,128)(2,1)S(1)}, bf16[64,4,256]{2,0,1:T(8,128)(2,1)S(1)}, u32[]{:S(2)}, u32[]{:S(2)}) collective-permute-start(bf16[64,4,256]{2,0,1:T(8,128)(2,1)S(1)} %get-tuple-element.41), channel_id=1, source_target_pairs={{2,0},{4,2},{6,4},{8,6},{10,8},{12,10},{14,12},{3,1},{5,3},{7,5},{... | collective-permute-start | bytes 393224 | tf_op jit(solution)/shard_map/ppermute | solution.py:19
  25.1 16.2 %collective-permute-start.2 = (bf16[64,72,4]{1,0,2:T(8,128)(2,1)}, bf16[64,72,4]{1,0,2:T(8,128)(2,1)}, u32[]{:S(2)}, u32[]{:S(2)}) collective-permute-start(bf16[64,72,4]{1,0,2:T(8,128)(2,1)} %copy.58), channel_id=1, source_target_pairs={{0,1},{2,3},{4,5},{6,7},{8,9},{10,11},{12,13},{14,15},{16,17},{18,... | collective-permute-start | bytes 110600 | tf_op jit(solution)/shard_map/ppermute | solution.py:17
  32.0 19.4 %collective-permute-start.3 = (bf16[64,72,4]{1,0,2:T(8,128)(2,1)}, bf16[64,72,4]{1,0,2:T(8,128)(2,1)}, u32[]{:S(2)}, u32[]{:S(2)}) collective-permute-start(bf16[64,72,4]{1,0,2:T(8,128)(2,1)} %copy.61), channel_id=1, source_target_pairs={{1,0},{3,2},{5,4},{7,6},{9,8},{11,10},{13,12},{15,14},{17,16},{19,... | collective-permute-start | bytes 110600 | tf_op jit(solution)/shard_map/ppermute | solution.py:19
  127.9 49.0 %all-to-all-start.1 = ((bf16[16,2,32768]{2,1,0:T(2,128)(2,1)}), bf16[16,2,32768]{2,1,0:T(2,128)(2,1)}, u32[]{:S(2)}, u32[]{:S(2)}) async-start(bf16[16,2,32768]{2,1,0:T(2,128)(2,1)} %reshape.99), calls=%async_computation.1 | async-start | bytes 4194304 | tf_op jit(solution)/shard_map/all_to_all | solution.py:50
  184.3 7.9 %copy-start.29 = (pred[32]{0:T(512)(128)(4,1)S(1)}, pred[32]{0:T(512)(128)(4,1)}, u32[]{:S(2)}) copy-start(pred[32]{0:T(512)(128)(4,1)} %copy-done.28) | copy-start | bytes 100
  184.3 8.6 %copy-start.25 = (f32[32,512]{1,0:T(8,128)S(1)}, f32[32,512]{1,0:T(8,128)}, u32[]{:S(2)}) copy-start(f32[32,512]{1,0:T(8,128)} %and_convert_fusion) | copy-start | bytes 196612
  184.3 8.6 %copy-start.27 = (s32[32,512]{1,0:T(8,128)S(1)}, s32[32,512]{1,0:T(8,128)}, u32[]{:S(2)}) copy-start(s32[32,512]{1,0:T(8,128)} %param.8) | copy-start | bytes 196612
  201.5 19.6 %all-to-all-start.2 = ((bf16[37,32,2,256]{3,1,0,2:T(8,128)(2,1)}), bf16[37,32,2,256]{3,1,0,2:T(8,128)(2,1)}, u32[]{:S(2)}, u32[]{:S(2)}) async-start(bf16[37,32,2,256]{3,1,0,2:T(8,128)(2,1)} %copy.72), calls=%async_computation.2 | async-start | bytes 2424832 | tf_op jit(solution)/shard_map/all_to_all | solution.py:38
  206.0 194.7 %all-reduce.3.cloned.1.call-start = ((), (), s32[]{:S(2)}) async-start(), calls=%async_computation.3 | async-start | bytes 589824 | tf_op jit(solution)/shard_map/psum | solution.py:135
  227.3 20.9 %copy-start.2 = (bf16[64,64,256]{2,0,1:T(8,128)(2,1)}, bf16[64,64,256]{2,0,1:T(8,128)(2,1)S(1)}, u32[]{:S(2)}) copy-start(bf16[64,64,256]{2,0,1:T(8,128)(2,1)S(1)} %get-tuple-element.48) | copy-start | bytes 6291460
  238.1 9.4 %copy-start.9 = (bf16[64,64,256]{2,0,1:T(8,128)(2,1)S(1)}, bf16[64,64,256]{2,0,1:T(8,128)(2,1)}, u32[]{:S(2)}) copy-start(bf16[64,64,256]{2,0,1:T(8,128)(2,1)} %copy-done.7) | copy-start | bytes 6291460
  238.1 9.4 %copy-start.24 = (bf16[64,4,256]{2,0,1:T(8,128)(2,1)S(1)}, bf16[64,4,256]{2,0,1:T(8,128)(2,1)}, u32[]{:S(2)}) copy-start(bf16[64,4,256]{2,0,1:T(8,128)(2,1)} %copy-done.23) | copy-start | bytes 393220
  241.7 71.4 %collective-permute-start.5 = (bf16[64,4,256]{2,0,1:T(8,128)(2,1)S(1)}, bf16[64,4,256]{2,0,1:T(8,128)(2,1)S(1)}, u32[]{:S(2)}, u32[]{:S(2)}) collective-permute-start(bf16[64,4,256]{2,0,1:T(8,128)(2,1)S(1)} %get-tuple-element.38), channel_id=1, source_target_pairs={{2,0},{4,2},{6,4},{8,6},{10,8},{12,10},{14,12},{3,1},{5,3},{7,5},{... | collective-permute-start | bytes 393224 | tf_op jit(solution)/shard_map/ppermute | solution.py:19
  243.0 70.1 %collective-permute-start.4 = (bf16[64,4,256]{2,0,1:T(8,128)(2,1)S(1)}, bf16[64,4,256]{2,0,1:T(8,128)(2,1)S(1)}, u32[]{:S(2)}, u32[]{:S(2)}) collective-permute-start(bf16[64,4,256]{2,0,1:T(8,128)(2,1)S(1)} %get-tuple-element.39), channel_id=1, source_target_pairs={{0,2},{2,4},{4,6},{6,8},{8,10},{10,12},{12,14},{1,3},{3,5},{5,7},{... | collective-permute-start | bytes 393224 | tf_op jit(solution)/shard_map/ppermute | solution.py:17
  318.0 12.0 %copy-start.3 = (bf16[64,64,256]{2,0,1:T(8,128)(2,1)S(1)}, bf16[64,64,256]{2,0,1:T(8,128)(2,1)}, u32[]{:S(2)}) copy-start(bf16[64,64,256]{2,0,1:T(8,128)(2,1)} %copy-done.2) | copy-start | bytes 6291460
  318.0 12.0 %copy-start.15 = (bf16[64,4,256]{2,0,1:T(8,128)(2,1)S(1)}, bf16[64,4,256]{2,0,1:T(8,128)(2,1)}, u32[]{:S(2)}) copy-start(bf16[64,4,256]{2,0,1:T(8,128)(2,1)} %copy-done.14) | copy-start | bytes 393220
  320.8 16.2 %collective-permute-start.6 = (bf16[64,72,4]{1,0,2:T(8,128)(2,1)S(1)}, bf16[64,72,4]{1,0,2:T(8,128)(2,1)}, u32[]{:S(2)}, u32[]{:S(2)}) collective-permute-start(bf16[64,72,4]{1,0,2:T(8,128)(2,1)S(1)} %copy.74), channel_id=1, source_target_pairs={{1,0},{3,2},{5,4},{7,6},{9,8},{11,10},{13,12},{15,14},{17,16},{19,... | collective-permute-start | bytes 110600 | tf_op jit(solution)/shard_map/ppermute | solution.py:19
  324.1 9.4 %copy-start.18 = (bf16[64,4,256]{2,0,1:T(8,128)(2,1)S(1)}, bf16[64,4,256]{2,0,1:T(8,128)(2,1)}, u32[]{:S(2)}) copy-start(bf16[64,4,256]{2,0,1:T(8,128)(2,1)} %copy-done.17) | copy-start | bytes 393220
  324.1 15.7 %collective-permute-start.7 = (bf16[64,72,4]{1,0,2:T(8,128)(2,1)}, bf16[64,72,4]{1,0,2:T(8,128)(2,1)}, u32[]{:S(2)}, u32[]{:S(2)}) collective-permute-start(bf16[64,72,4]{1,0,2:T(8,128)(2,1)} %copy.78), channel_id=1, source_target_pairs={{0,1},{2,3},{4,5},{6,7},{8,9},{10,11},{12,13},{14,15},{16,17},{18,... | collective-permute-start | bytes 110600 | tf_op jit(solution)/shard_map/ppermute | solution.py:17
  364.3 38.2 %copy-start.1 = (bf16[37,64]{1,0:T(8,128)(2,1)S(1)}, bf16[37,64]{1,0:T(8,128)(2,1)}, u32[]{:S(2)}) copy-start(bf16[37,64]{1,0:T(8,128)(2,1)} %param.12) | copy-start | bytes 14212
  (19 other events, 57.2 us)
Sparse Core Ops, SparseCore 0:
  313.2 87.4 all-reduce.2
where the time goes:
time: 418 us; the launch traced here: 411 us
  matrix products  113 us (27%)
  blocking collectives  92.3 us (22%)
  local copies, waits for them, and re-layouts  72.9 us (17%)
  waiting for transfers between devices  68.1 us (16%)
  starting transfers between devices  34.7 us (8%)
  between operations  17.4 us (4%)
  other arithmetic  12.7 us (3%)
    psum x1, blocking collectives, per_device(): lax.psum((conv_grad, conv_bias_grad, head_grad, head_bias_grad, loss_loca...  62.7 us
    dot_general x9, matrix products, per_device(): jnp.einsum('oc,cij->oij', conv_weight[offset_row, offset_column], sliding...  44.2 us
    dot_general x9, matrix products, per_device(): jnp.einsum('oc,oij->cij', conv_weight[offset_row, offset_column], source,...  35.5 us
    all_to_all x1, waiting for transfers between devices, mirror_features(): lax.all_to_all(blocks, ('row', 'col'), split_axis=2, concat_axis=2, tiled...  34 us
    all_to_all x1, blocking collectives, tile_to_band(): lax.all_to_all(split, 'col', split_axis=1, concat_axis=3, tiled=True)  29.7 us
    unnamed x71, local copies, waits for them, and re-layouts  27.2 us
    psum x1, waiting for transfers between devices, per_device(): lax.psum((conv_grad, conv_bias_grad, head_grad, head_bias_grad, loss_loca...  23.2 us
    ppermute x4, starting transfers between devices, with_halo(): lax.ppermute(tail, axis, [(i, (i + 1) % count) for i in range(ends)])  17.6 us
  transfers between devices with their start and end apart: 11, of which 3 were waited for; matrix products, arithmetic and copies ran while one was open for 23% of the time, Pallas kernels for 0%

commit v1 on v0

--- a/solution.py
+++ b/solution.py
@@ -4,6 +4,17 @@
 from jax.sharding import PartitionSpec as P
 
 DILATION_STEP = 4
+
+
+def in_blocks(x, dim, peers):
+    before, after = (x.shape[:dim], x.shape[dim + 1 :])
+    return jnp.moveaxis(x.reshape(*before, peers, -1, *after), dim, 0)
+
+
+def laid_out(pieces, dim):
+    pieces = jnp.moveaxis(pieces, 0, dim)
+    shape = pieces.shape
+    return pieces.reshape(*shape[:dim], shape[dim] * shape[dim + 1], *shape[dim + 2 :])
 
 
 def with_halo(cells, sides, width):
@@ -47,7 +58,17 @@
     channels, band_rows, length_cols = field.shape
     bands = lax.axis_size(("row", "col"))
     blocks = field.reshape(channels, band_rows, bands, band_rows)
-    moved = lax.all_to_all(blocks, ("row", "col"), split_axis=2, concat_axis=2, tiled=True)
+    size, index = (lax.axis_size(("row", "col")), lax.axis_index(("row", "col")))
+    pieces = in_blocks(blocks, 2, size)
+    filled = pieces
+    for hop in range(1, size):
+        target, source_2 = ((index + hop) % size, (index - hop) % size)
+        sent = lax.dynamic_index_in_dim(pieces, target, 0)
+        other = lax.ppermute(
+            sent, ("row", "col"), [(i_2, (i_2 + hop) % size) for i_2 in range(size)]
+        )
+        filled = lax.dynamic_update_slice_in_dim(filled, other, source_2, axis=0)
+    moved = laid_out(filled, 2)
     return reorder_back(moved, channels, band_rows, length_cols)
 
 

time: 418 us -> 448 us (1.072)
  starting transfers between devices: 34.7 us -> 95.7 us
  blocking collectives: 92.3 us -> 60 us
  waiting for transfers between devices: 68.1 us -> 88.9 us
  local copies, waits for them, and re-layouts: 72.9 us -> 60.5 us
  matrix products: 113 us -> 104 us
    ppermute x0 -> x15, starting transfers between devices: none -> 64.3 us  [mirror_features(): lax.ppermute(sent, ('row', 'col'), [(i_2, (i_2 + hop) % size) for i_2 in...]
    ppermute x0 -> x15, waiting for transfers between devices: none -> 35 us  [mirror_features(): lax.ppermute(sent, ('row', 'col'), [(i_2, (i_2 + hop) % size) for i_2 in...]
    all_to_all x1 -> x0, blocking collectives: 29.7 us -> none  [tile_to_band(): lax.all_to_all(split, 'col', split_axis=1, concat_axis=3, tiled=True)]
    unnamed x71 -> x64, local copies, waits for them, and re-layouts: 27.2 us -> 12.2 us
    all_to_all x1, waiting for transfers between devices: 34 us -> 23.7 us  [tile_to_band(): lax.all_to_all(split, 'col', split_axis=1, concat_axis=3, tiled=True)]
    another operation x1 -> x0, local copies, waits for them, and re-layouts: 5.31 us -> none  [mirror_features(): blocks = field.reshape(channels, band_rows, bands, band_rows)]
    dot_general x1, matrix products: 7.86 us -> 2.65 us  [per_device(): jnp.einsum('kc,cij->kij', head_weight, hidden_mirror, preferred_element_t...]
    all_to_all x1, waiting for transfers between devices: 10.8 us -> 6.06 us  [band_to_tile(): lax.all_to_all(split, 'col', split_axis=2, concat_axis=1, tiled=True)]
  transfers between devices with their start and end apart: 11 -> 26, of which waited for: 3 -> 7; matrix products, arithmetic and copies ran while one was open for 23% -> 21% of each run, Pallas kernels for 0% -> 0%
where the time goes in v1:
time: 448 us; the launch traced here: 440 us
  matrix products  104 us (23%)
  starting transfers between devices  95.7 us (21%)
  waiting for transfers between devices  88.9 us (20%)
  local copies, waits for them, and re-layouts  60.5 us (14%)
  blocking collectives  60 us (13%)
  between operations  18.3 us (4%)
  other arithmetic  12.7 us (3%)
    ppermute x15, starting transfers between devices, mirror_features(): lax.ppermute(sent, ('row', 'col'), [(i_2, (i_2 + hop) % size) for i_2 in...  64.3 us
    psum x1, blocking collectives, per_device(): lax.psum((conv_grad, conv_bias_grad, head_grad, head_bias_grad, loss_loca...  60 us
    dot_general x9, matrix products, per_device(): jnp.einsum('oc,cij->oij', conv_weight[offset_row, offset_column], sliding...  44.3 us
    dot_general x9, matrix products, per_device(): jnp.einsum('oc,oij->cij', conv_weight[offset_row, offset_column], source,...  35.6 us
    ppermute x15, waiting for transfers between devices, mirror_features(): lax.ppermute(sent, ('row', 'col'), [(i_2, (i_2 + hop) % size) for i_2 in...  35 us
    psum x1, waiting for transfers between devices, per_device(): lax.psum((conv_grad, conv_bias_grad, head_grad, head_bias_grad, loss_loca...  24.1 us
    all_to_all x1, waiting for transfers between devices, tile_to_band(): lax.all_to_all(split, 'col', split_axis=1, concat_axis=3, tiled=True)  23.7 us
    ppermute x4, starting transfers between devices, with_halo(): lax.ppermute(tail, axis, [(i, (i + 1) % count) for i in range(ends)])  16.4 us
  transfers between devices with their start and end apart: 26, of which 7 were waited for; matrix products, arithmetic and copies ran while one was open for 21% of the time, Pallas kernels for 0%

profile of v1, /device:TPU:0, one launch (start us, length us, event | category | flops | bytes accessed | tf_op | source)
XLA Modules:
  0.0 440.3 jit_solution(14428799395273393095)
XLA Ops:
  13.8 4.4 fusion.56
  25.1 4.9 %collective-permute-start.2 = (bf16[64,72,4]{1,0,2:T(8,128)(2,1)}, bf16[64,72,4]{1,0,2:T(8,128)(2,1)}, u32[]{:S(2)}, u32[]{:S(2)}) collective-permute-start(bf16[64,72,4]{1,0,2:T(8,128)(2,1)} %copy.58), channel_id=1, source_target_pairs={{0,1},{2,3},{4,5},{6,7},{8,9},{10,11},{12,13},{14,15},{16,17},{18,... | collective-permute-start | bytes 110600 | tf_op jit(solution)/shard_map/ppermute | solution.py:28
  33.6 4.3 fusion.37
  66.0 13.3 %fusion = (bf16[64,64,256]{2,0,1:T(8,128)(2,1)S(1)}, f32[64,64,256]{2,0,1:T(8,128)}) fusion(bf16[64,72,4]{2,0,1:T(8,128)(2,1)S(1)} %copy.62, bf16[64,72,256]{2,0,1:T(8,128)(2,1)S(1)} %constant_dynamic-update-slice_fusion, bf16[3,3,64,64]{3,2,1,0:T(8,128)(2,1)} %param.10, f32[64,256,64]{1,2,0:T(8,128)} %fusion.39, f32[64,256,64]{1,2,0:T(8,128)} %fusion.43, ...), kind=kOutput, calls=%fused_computation.6 | convolution fusion | flops 152043520 | bytes 42258688 | tf_op jit(solution)/shard_map/oc,cij->oij/dot_general | solution.py:89
  81.9 4.8 %all-to-all-start = ((bf16[64,2,32,256]{3,2,0,1:T(8,128)(2,1)}), bf16[64,2,32,256]{3,2,0,1:T(8,128)(2,1)}, u32[]{:S(2)}, u32[]{:S(2)}) async-start(bf16[64,2,32,256]{3,2,0,1:T(8,128)(2,1)} %copy.65), calls=%async_computation | async-start | bytes 4194304 | tf_op jit(solution)/shard_map/all_to_all | solution.py:41
  89.3 23.7 %all-to-all-done = bf16[64,2,32,256]{3,2,0,1:T(8,128)(2,1)} async-done(((bf16[64,2,32,256]{3,2,0,1:T(8,128)(2,1)}), bf16[64,2,32,256]{3,2,0,1:T(8,128)(2,1)}, u32[]{:S(2)}, u32[]{:S(2)}) %all-to-all-start) | async-done | bytes 2097184 | tf_op jit(solution)/shard_map/all_to_all | solution.py:41
  113.0 5.0 %copy.66 = bf16[64,2,32,256]{0,3,1,2:T(8,128)(2,1)} copy(bf16[64,2,32,256]{3,2,0,1:T(8,128)(2,1)} %all-to-all-done) | data formatting | bytes 4194304 | tf_op jit(solution)/shard_map/all_to_all | solution.py:41
  125.9 4.2 collective-permute-start.6
  141.1 4.9 %collective-permute-start.12 = (bf16[1,64,32,1,32]{1,4,0,2,3:T(8,128)(2,1)S(1)}, bf16[1,64,32,1,32]{1,4,0,2,3:T(8,128)(2,1)S(1)}, u32[]{:S(2)}, u32[]{:S(2)}) collective-permute-start(bf16[1,64,32,1,32]{1,4,0,2,3:T(8,128)(2,1)S(1)} %get-tuple-element.38), channel_id=1, source_target_pairs={{0,9},{1,10},{2,11},{3,12},{4,13},{5,14},{6,15},{7,0},{8,1},{9,2},... | collective-permute-start | bytes 393224 | tf_op jit(solution)/shard_map/ppermute | solution.py:67
  146.0 28.4 %collective-permute-done.8 = bf16[1,64,32,1,32]{1,4,0,2,3:T(8,128)(2,1)S(1)} collective-permute-done((bf16[1,64,32,1,32]{1,4,0,2,3:T(8,128)(2,1)S(1)}, bf16[1,64,32,1,32]{1,4,0,2,3:T(8,128)(2,1)S(1)}, u32[]{:S(2)}, u32[]{:S(2)}) %collective-permute-start.8) | collective-permute-done | bytes 131104 | tf_op jit(solution)/shard_map/ppermute | solution.py:67
  176.7 13.6 %collective-permute-start.14 = (bf16[1,64,32,1,32]{1,4,0,2,3:T(8,128)(2,1)S(1)}, bf16[1,64,32,1,32]{1,4,0,2,3:T(8,128)(2,1)S(1)}, u32[]{:S(2)}, u32[]{:S(2)}) collective-permute-start(bf16[1,64,32,1,32]{1,4,0,2,3:T(8,128)(2,1)S(1)} %get-tuple-element.36), channel_id=1, source_target_pairs={{0,11},{1,12},{2,13},{3,14},{4,15},{5,0},{6,1},{7,2},{8,3},{9,4},{... | collective-permute-start | bytes 393224 | tf_op jit(solution)/shard_map/ppermute | solution.py:67
  190.4 12.7 %collective-permute-start.15 = (bf16[1,64,32,1,32]{1,4,0,2,3:T(8,128)(2,1)S(1)}, bf16[1,64,32,1,32]{1,4,0,2,3:T(8,128)(2,1)S(1)}, u32[]{:S(2)}, u32[]{:S(2)}) collective-permute-start(bf16[1,64,32,1,32]{1,4,0,2,3:T(8,128)(2,1)S(1)} %get-tuple-element.35), channel_id=1, source_target_pairs={{0,12},{1,13},{2,14},{3,15},{4,0},{5,1},{6,2},{7,3},{8,4},{9,5},{1... | collective-permute-start | bytes 393224 | tf_op jit(solution)/shard_map/ppermute | solution.py:67
  203.1 5.6 %collective-permute-start.16 = (bf16[1,64,32,1,32]{1,4,0,2,3:T(8,128)(2,1)S(1)}, bf16[1,64,32,1,32]{1,4,0,2,3:T(8,128)(2,1)S(1)}, u32[]{:S(2)}, u32[]{:S(2)}) collective-permute-start(bf16[1,64,32,1,32]{1,4,0,2,3:T(8,128)(2,1)S(1)} %get-tuple-element.34), channel_id=1, source_target_pairs={{0,13},{1,14},{2,15},{3,0},{4,1},{5,2},{6,3},{7,4},{8,5},{9,6},{10... | collective-permute-start | bytes 393224 | tf_op jit(solution)/shard_map/ppermute | solution.py:67
  208.7 6.1 %collective-permute-start.17 = (bf16[1,64,32,1,32]{1,4,0,2,3:T(8,128)(2,1)S(1)}, bf16[1,64,32,1,32]{1,4,0,2,3:T(8,128)(2,1)S(1)}, u32[]{:S(2)}, u32[]{:S(2)}) collective-permute-start(bf16[1,64,32,1,32]{1,4,0,2,3:T(8,128)(2,1)S(1)} %get-tuple-element.33), channel_id=1, source_target_pairs={{0,14},{1,15},{2,0},{3,1},{4,2},{5,3},{6,4},{7,5},{8,6},{9,7},{10,... | collective-permute-start | bytes 393224 | tf_op jit(solution)/shard_map/ppermute | solution.py:67
  214.8 6.0 %collective-permute-start.18 = (bf16[1,64,32,1,32]{1,4,0,2,3:T(8,128)(2,1)S(1)}, bf16[1,64,32,1,32]{1,4,0,2,3:T(8,128)(2,1)S(1)}, u32[]{:S(2)}, u32[]{:S(2)}) collective-permute-start(bf16[1,64,32,1,32]{1,4,0,2,3:T(8,128)(2,1)S(1)} %get-tuple-element.32), channel_id=1, source_target_pairs={{0,15},{1,0},{2,1},{3,2},{4,3},{5,4},{6,5},{7,6},{8,7},{9,8},{10,9... | collective-permute-start | bytes 393224 | tf_op jit(solution)/shard_map/ppermute | solution.py:67
  239.5 4.5 %all-to-all-start.1 = ((bf16[37,32,2,256]{3,1,0,2:T(8,128)(2,1)}), bf16[37,32,2,256]{3,1,0,2:T(8,128)(2,1)}, u32[]{:S(2)}, u32[]{:S(2)}) async-start(bf16[37,32,2,256]{3,1,0,2:T(8,128)(2,1)} %copy.71), calls=%async_computation.1 | async-start | bytes 2424832 | tf_op jit(solution)/shard_map/all_to_all | solution.py:49
  244.2 4.1 convolution_bitcast_fusion.7
  248.2 6.1 %all-to-all-done.1 = bf16[37,32,2,256]{3,1,0,2:T(8,128)(2,1)} async-done(((bf16[37,32,2,256]{3,1,0,2:T(8,128)(2,1)}), bf16[37,32,2,256]{3,1,0,2:T(8,128)(2,1)}, u32[]{:S(2)}, u32[]{:S(2)}) %all-to-all-start.1) | async-done | bytes 1212448 | tf_op jit(solution)/shard_map/all_to_all | solution.py:49
  256.3 4.2 convert_reduce_fusion
  281.1 60.0 %all-reduce = (f32[64]{0:T(128)}, f32[37,64]{1,0:T(8,128)}, f32[37]{0:T(128)}, f32[]{:T(128)}) all-reduce(f32[64]{0:T(128)S(1)} %copy-done.27, f32[37,64]{1,0:T(8,128)S(1)} %copy-done.23, f32[37]{0:T(128)S(1)} %get-tuple-element.30, f32[]{:T(128)} %get-tuple-element.57), channel_id=1, replica_groups=mesh['parts'=2,'row'=8,'col'=2] {'row','col'}, use_global_device_ids=true, to_apply=%region_3.4 | all-reduce | flops 2470 | bytes 19760 | tf_op jit(solution)/shard_map/psum | solution.py:156
  352.7 5.8 %collective-permute-start.22 = (bf16[64,72,4]{1,0,2:T(8,128)(2,1)}, bf16[64,72,4]{1,0,2:T(8,128)(2,1)}, u32[]{:S(2)}, u32[]{:S(2)}) collective-permute-start(bf16[64,72,4]{1,0,2:T(8,128)(2,1)} %copy.77), channel_id=1, source_target_pairs={{0,1},{2,3},{4,5},{6,7},{8,9},{10,11},{12,13},{14,15},{16,17},{18,... | collective-permute-start | bytes 110600 | tf_op jit(solution)/shard_map/ppermute | solution.py:28
  372.0 6.5 %maximum_maximum_fusion = (bf16[64,72,260]{2,0,1:T(8,128)(2,1)S(1)}, bf16[64,72,260]{2,0,1:T(8,128)(2,1)S(1)}) fusion(bf16[64,4,256]{2,0,1:T(8,128)(2,1)S(1)} %collective-permute-done.20, bf16[64,64,256]{2,0,1:T(8,128)(2,1)S(1)} %copy-done.3, bf16[64,4,256]{2,0,1:T(8,128)(2,1)S(1)} %collective-permute-done.19, bf16[64,72,4]{2,0,1:T(8,128)(2,1)} %copy.78, ...), kind=kLoop, calls=%fused_computation.21 | loop fusion | flops 19169280 | bytes 7225344 | tf_op jit(solution)/shard_map/concatenate | solution.py:26
  392.8 10.8 %fusion.22 = bf16[64,64,256]{2,0,1:T(8,128)(2,1)S(1)} fusion(f32[64,256,64]{1,2,0:T(8,128)} %fusion.14, f32[64,256,64]{1,2,0:T(8,128)} %fusion.27, f32[64,256,64]{1,2,0:T(8,128)} %fusion.29, f32[64,256,64]{1,2,0:T(8,128)S(1)} %copy-done.13, f32[64,256,64]{1,2,0:T(8,128)} %fusion.31, f32[64,256,64]{1,2,0:T(8,128)} %fusion.33, f32[64,256,64]{1,2,0:T(8,128)} %fusion.35, ...), kind=kOutput, calls=%fused_computation.48 | convolution fusion | flops 143654912 | bytes 37765120 | tf_op jit(solution)/shard_map/oc,oij->cij/dot_general | solution.py:147
  406.1 24.1 %all-reduce.3.cloned.1.call-done = f32[3,3,64,64]{3,2,1,0:T(8,128)} async-done(((f32[3,3,64,64]{3,2,1,0:T(8,128)}), f32[3,3,64,64]{3,2,1,0:T(8,128)}) %all-reduce.3.cloned.1.call-update) | async-done | bytes 147472 | tf_op jit(solution)/shard_map/psum | solution.py:156
  (170 shorter events, 154.4 us)
Async XLA Ops:
  25.1 16.3 %collective-permute-start.2 = (bf16[64,72,4]{1,0,2:T(8,128)(2,1)}, bf16[64,72,4]{1,0,2:T(8,128)(2,1)}, u32[]{:S(2)}, u32[]{:S(2)}) collective-permute-start(bf16[64,72,4]{1,0,2:T(8,128)(2,1)} %copy.58), channel_id=1, source_target_pairs={{0,1},{2,3},{4,5},{6,7},{8,9},{10,11},{12,13},{14,15},{16,17},{18,... | collective-permute-start | bytes 110600 | tf_op jit(solution)/shard_map/ppermute | solution.py:28
  32.0 19.5 %collective-permute-start.3 = (bf16[64,72,4]{1,0,2:T(8,128)(2,1)}, bf16[64,72,4]{1,0,2:T(8,128)(2,1)}, u32[]{:S(2)}, u32[]{:S(2)}) collective-permute-start(bf16[64,72,4]{1,0,2:T(8,128)(2,1)} %copy.61), channel_id=1, source_target_pairs={{1,0},{3,2},{5,4},{7,6},{9,8},{11,10},{13,12},{15,14},{17,16},{19,... | collective-permute-start | bytes 110600 | tf_op jit(solution)/shard_map/ppermute | solution.py:30
  81.9 31.1 %all-to-all-start = ((bf16[64,2,32,256]{3,2,0,1:T(8,128)(2,1)}), bf16[64,2,32,256]{3,2,0,1:T(8,128)(2,1)}, u32[]{:S(2)}, u32[]{:S(2)}) async-start(bf16[64,2,32,256]{3,2,0,1:T(8,128)(2,1)} %copy.65), calls=%async_computation | async-start | bytes 4194304 | tf_op jit(solution)/shard_map/all_to_all | solution.py:41
  121.0 11.1 %collective-permute-start.4 = (bf16[1,64,32,1,32]{1,4,0,2,3:T(8,128)(2,1)S(1)}, bf16[1,64,32,1,32]{1,4,0,2,3:T(8,128)(2,1)S(1)}, u32[]{:S(2)}, u32[]{:S(2)}) collective-permute-start(bf16[1,64,32,1,32]{1,4,0,2,3:T(8,128)(2,1)S(1)} %get-tuple-element.46), channel_id=1, source_target_pairs={{0,1},{1,2},{2,3},{3,4},{4,5},{5,6},{6,7},{7,8},{8,9},{9,10},{10,1... | collective-permute-start | bytes 393224 | tf_op jit(solution)/shard_map/ppermute | solution.py:67
  121.1 12.7 %collective-permute-start.5 = (bf16[1,64,32,1,32]{1,4,0,2,3:T(8,128)(2,1)S(1)}, bf16[1,64,32,1,32]{1,4,0,2,3:T(8,128)(2,1)S(1)}, u32[]{:S(2)}, u32[]{:S(2)}) collective-permute-start(bf16[1,64,32,1,32]{1,4,0,2,3:T(8,128)(2,1)S(1)} %get-tuple-element.45), channel_id=1, source_target_pairs={{0,2},{1,3},{2,4},{3,5},{4,6},{5,7},{6,8},{7,9},{8,10},{9,11},{10,... | collective-permute-start | bytes 393224 | tf_op jit(solution)/shard_map/ppermute | solution.py:67
  125.9 10.6 %collective-permute-start.6 = (bf16[1,64,32,1,32]{1,4,0,2,3:T(8,128)(2,1)S(1)}, bf16[1,64,32,1,32]{1,4,0,2,3:T(8,128)(2,1)S(1)}, u32[]{:S(2)}, u32[]{:S(2)}) collective-permute-start(bf16[1,64,32,1,32]{1,4,0,2,3:T(8,128)(2,1)S(1)} %get-tuple-element.44), channel_id=1, source_target_pairs={{0,3},{1,4},{2,5},{3,6},{4,7},{5,8},{6,9},{7,10},{8,11},{9,12},{10... | collective-permute-start | bytes 393224 | tf_op jit(solution)/shard_map/ppermute | solution.py:67
  130.1 11.0 %collective-permute-start.7 = (bf16[1,64,32,1,32]{1,4,0,2,3:T(8,128)(2,1)S(1)}, bf16[1,64,32,1,32]{1,4,0,2,3:T(8,128)(2,1)S(1)}, u32[]{:S(2)}, u32[]{:S(2)}) collective-permute-start(bf16[1,64,32,1,32]{1,4,0,2,3:T(8,128)(2,1)S(1)} %get-tuple-element.43), channel_id=1, source_target_pairs={{0,4},{1,5},{2,6},{3,7},{4,8},{5,9},{6,10},{7,11},{8,12},{9,13},{1... | collective-permute-start | bytes 393224 | tf_op jit(solution)/shard_map/ppermute | solution.py:67
  131.6 42.7 %collective-permute-start.8 = (bf16[1,64,32,1,32]{1,4,0,2,3:T(8,128)(2,1)S(1)}, bf16[1,64,32,1,32]{1,4,0,2,3:T(8,128)(2,1)S(1)}, u32[]{:S(2)}, u32[]{:S(2)}) collective-permute-start(bf16[1,64,32,1,32]{1,4,0,2,3:T(8,128)(2,1)S(1)} %get-tuple-element.42), channel_id=1, source_target_pairs={{0,5},{1,6},{2,7},{3,8},{4,9},{5,10},{6,11},{7,12},{8,13},{9,14},{... | collective-permute-start | bytes 393224 | tf_op jit(solution)/shard_map/ppermute | solution.py:67
  132.1 44.6 %collective-permute-start.9 = (bf16[1,64,32,1,32]{1,4,0,2,3:T(8,128)(2,1)S(1)}, bf16[1,64,32,1,32]{1,4,0,2,3:T(8,128)(2,1)S(1)}, u32[]{:S(2)}, u32[]{:S(2)}) collective-permute-start(bf16[1,64,32,1,32]{1,4,0,2,3:T(8,128)(2,1)S(1)} %get-tuple-element.41), channel_id=1, source_target_pairs={{0,6},{1,7},{2,8},{3,9},{4,10},{5,11},{6,12},{7,13},{8,14},{9,15},... | collective-permute-start | bytes 393224 | tf_op jit(solution)/shard_map/ppermute | solution.py:67
  133.7 56.7 %collective-permute-start.10 = (bf16[1,64,32,1,32]{1,4,0,2,3:T(8,128)(2,1)S(1)}, bf16[1,64,32,1,32]{1,4,0,2,3:T(8,128)(2,1)S(1)}, u32[]{:S(2)}, u32[]{:S(2)}) collective-permute-start(bf16[1,64,32,1,32]{1,4,0,2,3:T(8,128)(2,1)S(1)} %get-tuple-element.40), channel_id=1, source_target_pairs={{0,7},{1,8},{2,9},{3,10},{4,11},{5,12},{6,13},{7,14},{8,15},{9,0},... | collective-permute-start | bytes 393224 | tf_op jit(solution)/shard_map/ppermute | solution.py:67
  136.5 66.6 %collective-permute-start.11 = (bf16[1,64,32,1,32]{1,4,0,2,3:T(8,128)(2,1)S(1)}, bf16[1,64,32,1,32]{1,4,0,2,3:T(8,128)(2,1)S(1)}, u32[]{:S(2)}, u32[]{:S(2)}) collective-permute-start(bf16[1,64,32,1,32]{1,4,0,2,3:T(8,128)(2,1)S(1)} %get-tuple-element.39), channel_id=1, source_target_pairs={{0,8},{1,9},{2,10},{3,11},{4,12},{5,13},{6,14},{7,15},{8,0},{9,1},... | collective-permute-start | bytes 393224 | tf_op jit(solution)/shard_map/ppermute | solution.py:67
  141.1 67.6 %collective-permute-start.12 = (bf16[1,64,32,1,32]{1,4,0,2,3:T(8,128)(2,1)S(1)}, bf16[1,64,32,1,32]{1,4,0,2,3:T(8,128)(2,1)S(1)}, u32[]{:S(2)}, u32[]{:S(2)}) collective-permute-start(bf16[1,64,32,1,32]{1,4,0,2,3:T(8,128)(2,1)S(1)} %get-tuple-element.38), channel_id=1, source_target_pairs={{0,9},{1,10},{2,11},{3,12},{4,13},{5,14},{6,15},{7,0},{8,1},{9,2},... | collective-permute-start | bytes 393224 | tf_op jit(solution)/shard_map/ppermute | solution.py:67
  174.4 40.4 %collective-permute-start.13 = (bf16[1,64,32,1,32]{1,4,0,2,3:T(8,128)(2,1)S(1)}, bf16[1,64,32,1,32]{1,4,0,2,3:T(8,128)(2,1)S(1)}, u32[]{:S(2)}, u32[]{:S(2)}) collective-permute-start(bf16[1,64,32,1,32]{1,4,0,2,3:T(8,128)(2,1)S(1)} %get-tuple-element.37), channel_id=1, source_target_pairs={{0,10},{1,11},{2,12},{3,13},{4,14},{5,15},{6,0},{7,1},{8,2},{9,3},... | collective-permute-start | bytes 393224 | tf_op jit(solution)/shard_map/ppermute | solution.py:67
  176.7 44.1 %collective-permute-start.14 = (bf16[1,64,32,1,32]{1,4,0,2,3:T(8,128)(2,1)S(1)}, bf16[1,64,32,1,32]{1,4,0,2,3:T(8,128)(2,1)S(1)}, u32[]{:S(2)}, u32[]{:S(2)}) collective-permute-start(bf16[1,64,32,1,32]{1,4,0,2,3:T(8,128)(2,1)S(1)} %get-tuple-element.36), channel_id=1, source_target_pairs={{0,11},{1,12},{2,13},{3,14},{4,15},{5,0},{6,1},{7,2},{8,3},{9,4},{... | collective-permute-start | bytes 393224 | tf_op jit(solution)/shard_map/ppermute | solution.py:67
  190.4 30.5 %collective-permute-start.15 = (bf16[1,64,32,1,32]{1,4,0,2,3:T(8,128)(2,1)S(1)}, bf16[1,64,32,1,32]{1,4,0,2,3:T(8,128)(2,1)S(1)}, u32[]{:S(2)}, u32[]{:S(2)}) collective-permute-start(bf16[1,64,32,1,32]{1,4,0,2,3:T(8,128)(2,1)S(1)} %get-tuple-element.35), channel_id=1, source_target_pairs={{0,12},{1,13},{2,14},{3,15},{4,0},{5,1},{6,2},{7,3},{8,4},{9,5},{1... | collective-permute-start | bytes 393224 | tf_op jit(solution)/shard_map/ppermute | solution.py:67
  203.1 17.9 %collective-permute-start.16 = (bf16[1,64,32,1,32]{1,4,0,2,3:T(8,128)(2,1)S(1)}, bf16[1,64,32,1,32]{1,4,0,2,3:T(8,128)(2,1)S(1)}, u32[]{:S(2)}, u32[]{:S(2)}) collective-permute-start(bf16[1,64,32,1,32]{1,4,0,2,3:T(8,128)(2,1)S(1)} %get-tuple-element.34), channel_id=1, source_target_pairs={{0,13},{1,14},{2,15},{3,0},{4,1},{5,2},{6,3},{7,4},{8,5},{9,6},{10... | collective-permute-start | bytes 393224 | tf_op jit(solution)/shard_map/ppermute | solution.py:67
  208.7 12.3 %collective-permute-start.17 = (bf16[1,64,32,1,32]{1,4,0,2,3:T(8,128)(2,1)S(1)}, bf16[1,64,32,1,32]{1,4,0,2,3:T(8,128)(2,1)S(1)}, u32[]{:S(2)}, u32[]{:S(2)}) collective-permute-start(bf16[1,64,32,1,32]{1,4,0,2,3:T(8,128)(2,1)S(1)} %get-tuple-element.33), channel_id=1, source_target_pairs={{0,14},{1,15},{2,0},{3,1},{4,2},{5,3},{6,4},{7,5},{8,6},{9,7},{10,... | collective-permute-start | bytes 393224 | tf_op jit(solution)/shard_map/ppermute | solution.py:67
  214.8 9.8 %collective-permute-start.18 = (bf16[1,64,32,1,32]{1,4,0,2,3:T(8,128)(2,1)S(1)}, bf16[1,64,32,1,32]{1,4,0,2,3:T(8,128)(2,1)S(1)}, u32[]{:S(2)}, u32[]{:S(2)}) collective-permute-start(bf16[1,64,32,1,32]{1,4,0,2,3:T(8,128)(2,1)S(1)} %get-tuple-element.32), channel_id=1, source_target_pairs={{0,15},{1,0},{2,1},{3,2},{4,3},{5,4},{6,5},{7,6},{8,7},{9,8},{10,9... | collective-permute-start | bytes 393224 | tf_op jit(solution)/shard_map/ppermute | solution.py:67
  239.5 14.8 %all-to-all-start.1 = ((bf16[37,32,2,256]{3,1,0,2:T(8,128)(2,1)}), bf16[37,32,2,256]{3,1,0,2:T(8,128)(2,1)}, u32[]{:S(2)}, u32[]{:S(2)}) async-start(bf16[37,32,2,256]{3,1,0,2:T(8,128)(2,1)} %copy.71), calls=%async_computation.1 | async-start | bytes 2424832 | tf_op jit(solution)/shard_map/all_to_all | solution.py:49
  243.9 186.3 %all-reduce.3.cloned.1.call-start = ((), (), s32[]{:S(2)}) async-start(), calls=%async_computation.2 | async-start | bytes 589824 | tf_op jit(solution)/shard_map/psum | solution.py:156
  274.9 67.7 %collective-permute-start.20 = (bf16[64,4,256]{2,0,1:T(8,128)(2,1)S(1)}, bf16[64,4,256]{2,0,1:T(8,128)(2,1)S(1)}, u32[]{:S(2)}, u32[]{:S(2)}) collective-permute-start(bf16[64,4,256]{2,0,1:T(8,128)(2,1)S(1)} %get-tuple-element.53), channel_id=1, source_target_pairs={{2,0},{4,2},{6,4},{8,6},{10,8},{12,10},{14,12},{3,1},{5,3},{7,5},{... | collective-permute-start | bytes 393224 | tf_op jit(solution)/shard_map/ppermute | solution.py:30
  276.2 66.4 %collective-permute-start.19 = (bf16[64,4,256]{2,0,1:T(8,128)(2,1)S(1)}, bf16[64,4,256]{2,0,1:T(8,128)(2,1)S(1)}, u32[]{:S(2)}, u32[]{:S(2)}) collective-permute-start(bf16[64,4,256]{2,0,1:T(8,128)(2,1)S(1)} %get-tuple-element.54), channel_id=1, source_target_pairs={{0,2},{2,4},{4,6},{6,8},{8,10},{10,12},{12,14},{1,3},{3,5},{5,7},{... | collective-permute-start | bytes 393224 | tf_op jit(solution)/shard_map/ppermute | solution.py:28
  349.4 16.1 %collective-permute-start.21 = (bf16[64,72,4]{1,0,2:T(8,128)(2,1)}, bf16[64,72,4]{1,0,2:T(8,128)(2,1)}, u32[]{:S(2)}, u32[]{:S(2)}) collective-permute-start(bf16[64,72,4]{1,0,2:T(8,128)(2,1)} %copy.73), channel_id=1, source_target_pairs={{1,0},{3,2},{5,4},{7,6},{9,8},{11,10},{13,12},{15,14},{17,16},{19,... | collective-permute-start | bytes 110600 | tf_op jit(solution)/shard_map/ppermute | solution.py:30
  352.7 15.6 %collective-permute-start.22 = (bf16[64,72,4]{1,0,2:T(8,128)(2,1)}, bf16[64,72,4]{1,0,2:T(8,128)(2,1)}, u32[]{:S(2)}, u32[]{:S(2)}) collective-permute-start(bf16[64,72,4]{1,0,2:T(8,128)(2,1)} %copy.77), channel_id=1, source_target_pairs={{0,1},{2,3},{4,5},{6,7},{8,9},{10,11},{12,13},{14,15},{16,17},{18,... | collective-permute-start | bytes 110600 | tf_op jit(solution)/shard_map/ppermute | solution.py:28
  (31 other events, 298.4 us)
Sparse Core Ops, SparseCore 0:
  342.7 87.4 all-reduce.2
